TPU v7x, 32 devices: a whole 2x2x4 slice. The times are simulated.
32 devices in a mesh: dp: 8 (over z, x), mp: 4 (over y, core).
Axes of the slice: x: 2, y: 2, z: 4, core: 2. Of those that a mesh axis runs over, the one named last changes fastest.
Arguments:
- text_blocks: bfloat16 [256, 64, 768], P(('dp', 'mp')), may hold values from -6 to 6
- visual_blocks: bfloat16 [256, 40, 768], P(('dp', 'mp')), may hold values from -6 to 6
- drop_flags: int32 [256, 2], P('dp'), may hold values 0 or 1
- qkv_weight: bfloat16 [4, 768, 3, 768], P(None, None, None, 'mp'), may hold values from -0.21875 to 0.21875
- out_weight: bfloat16 [4, 768, 768], P(None, 'mp'), may hold values from -0.625 to 0.625
- up_weight: bfloat16 [2, 768, 3072], P(None, None, 'mp'), may hold values from -0.21875 to 0.21875
- down_weight: bfloat16 [2, 3072, 768], P(None, 'mp'), may hold values from -0.109375 to 0.109375
- norm_gain: float32 [6, 768], replicated, may hold values from 0.5 to 1.5
- norm_shift: float32 [6, 768], replicated, may hold values from -3 to 3
- text_cotangent: bfloat16 [256, 64, 768], P(('dp', 'mp')), may hold values from -6 to 6
- visual_cotangent: bfloat16 [256, 40, 768], P(('dp', 'mp')), may hold values from -6 to 6
Outputs:
- text_output: bfloat16 [256, 64, 768], P(('dp', 'mp'))
- visual_output: bfloat16 [256, 40, 768], P(('dp', 'mp'))
- text_gradient: bfloat16 [256, 64, 768], P(('dp', 'mp'))
- visual_gradient: bfloat16 [256, 40, 768], P(('dp', 'mp'))
- qkv_gradient: float32 [4, 768, 3, 768], P(None, None, None, 'mp')
- out_gradient: float32 [4, 768, 768], P(None, 'mp')
- up_gradient: float32 [2, 768, 3072], P(None, None, 'mp')
- down_gradient: float32 [2, 3072, 768], P(None, 'mp')
- gain_gradient: float32 [6, 768], replicated
- shift_gradient: float32 [6, 768], replicated
Inputs may be any that keep to these rules, and one draw needn't show every extreme that they name: drop_flags[:, 0] = 1 marks a page whose text is absent, drop_flags[:, 1] = 1 one whose visual blocks are absent.
All inputs are finite; a program needn't handle non-finite values.
Results may differ from a plain program's by a relative error of at most 0.025.
Values may be sent and summed in bfloat16 or wider, within the bound.
No kernel may reach another device: no remote copies, remote signals or barrier semaphores. Data moves between devices by JAX's collectives and lax.ppermute only.
A program may use at most 256 MiB of HBM per device.

v0:
```python
import jax
import jax.numpy as jnp
from jax import lax
from jax.sharding import PartitionSpec as P

HEAD = 64
EPSILON = 1e-05


def normalize(values, gain, shift):
    center = values - jnp.mean(values, axis=-1, keepdims=True)
    spread = jnp.mean(center * center, axis=-1, keepdims=True)
    return center * lax.rsqrt(spread + EPSILON) * gain + shift


def linear(activation, weight):
    return jnp.einsum("pld,de->ple", activation, weight, preferred_element_type=jnp.float32)


def linear_back(gradient, weight):
    return jnp.einsum("ple,de->pld", gradient, weight, preferred_element_type=jnp.float32)


def weight_grad(activation, gradient):
    return jnp.einsum("pld,ple->de", activation, gradient, preferred_element_type=jnp.float32)


def split_heads(values):
    return values.reshape(values.shape[0], values.shape[1], values.shape[2] // HEAD, HEAD)


def merge_heads(values):
    return values.reshape(values.shape[0], values.shape[1], values.shape[2] * values.shape[3])


def score_block(queries, key_block):
    raw = jnp.einsum(
        "pqhe,pkhe->phqk",
        split_heads(queries),
        split_heads(key_block),
        preferred_element_type=jnp.float32,
    )
    return raw * HEAD ** (-0.5)


def attend_context(query_side, key_side, weight_block, keep_mask):
    queries = linear(query_side, weight_block[:, 0]).astype(jnp.bfloat16)
    key_block = linear(key_side, weight_block[:, 1]).astype(jnp.bfloat16)
    value_block = linear(key_side, weight_block[:, 2]).astype(jnp.bfloat16)
    scores = score_block(queries, key_block)
    row_max = jnp.max(scores, axis=-1, keepdims=True)
    log_total = row_max + jnp.log(jnp.sum(jnp.exp(scores - row_max), axis=-1, keepdims=True))
    probability = jnp.exp(scores - log_total).astype(jnp.bfloat16)
    context = merge_heads(
        jnp.einsum(
            "phqk,pkhe->pqhe",
            probability,
            split_heads(value_block),
            preferred_element_type=jnp.float32,
        )
    )
    if keep_mask is not None:
        context = context * keep_mask[:, None, None]
    context = context.astype(jnp.bfloat16)
    return (context, (queries, key_block, value_block, log_total, context))


def attend_back(query_side, key_side, weight_block, out_block, keep_mask, saved, out_grad):
    queries, key_block, value_block, log_total, context = saved
    out_weight_grad = weight_grad(context, out_grad)
    context_grad = linear_back(out_grad, out_block).astype(jnp.bfloat16)
    if keep_mask is not None:
        context_grad = context_grad * keep_mask[:, None, None].astype(jnp.bfloat16)
    probability = jnp.exp(score_block(queries, key_block) - log_total)
    heads_grad = split_heads(context_grad)
    prob_grad = jnp.einsum(
        "pqhe,pkhe->phqk", heads_grad, split_heads(value_block), preferred_element_type=jnp.float32
    )
    value_grad = merge_heads(
        jnp.einsum(
            "phqk,pqhe->pkhe",
            probability.astype(jnp.bfloat16),
            heads_grad,
            preferred_element_type=jnp.float32,
        )
    ).astype(jnp.bfloat16)
    score_grad = (
        probability * (prob_grad - jnp.sum(prob_grad * probability, axis=-1, keepdims=True))
    ).astype(jnp.bfloat16)
    query_grad = (
        merge_heads(
            jnp.einsum(
                "phqk,pkhe->pqhe",
                score_grad,
                split_heads(key_block),
                preferred_element_type=jnp.float32,
            )
        )
        * HEAD ** (-0.5)
    ).astype(jnp.bfloat16)
    key_grad = (
        merge_heads(
            jnp.einsum(
                "phqk,pqhe->pkhe",
                score_grad,
                split_heads(queries),
                preferred_element_type=jnp.float32,
            )
        )
        * HEAD ** (-0.5)
    ).astype(jnp.bfloat16)
    in_weight_grad = jnp.stack(
        [
            weight_grad(query_side, query_grad),
            weight_grad(key_side, key_grad),
            weight_grad(key_side, value_grad),
        ],
        axis=1,
    )
    query_back = linear_back(query_grad, weight_block[:, 0])
    key_back = linear_back(key_grad, weight_block[:, 1]) + linear_back(
        value_grad, weight_block[:, 2]
    )
    return (in_weight_grad, out_weight_grad, query_back, key_back)


def feed_forward(activation, up_block, down_block):
    before = linear(activation, up_block)
    hidden = jax.nn.gelu(before).astype(jnp.bfloat16)
    return (linear(hidden, down_block), (before, hidden))


def feed_back(activation, up_block, down_block, saved, out_grad):
    before, hidden = saved
    down_grad = weight_grad(hidden, out_grad)
    hidden_grad = linear_back(out_grad, down_block)
    gelu_pull = jax.vjp(jax.nn.gelu, before)[1]
    before_grad = gelu_pull(hidden_grad)[0].astype(jnp.bfloat16)
    up_grad = weight_grad(activation, before_grad)
    return (up_grad, down_grad, linear_back(before_grad, up_block))


def per_device(
    text_blocks,
    visual_blocks,
    drop_flags,
    qkv_weight,
    out_weight,
    up_weight,
    down_weight,
    norm_gain,
    norm_shift,
    text_cotangent,
    visual_cotangent,
):
    keep_text = (1 - drop_flags[:, 0]).astype(jnp.float32)
    keep_visual = (1 - drop_flags[:, 1]).astype(jnp.float32)
    text_now = text_blocks.astype(jnp.float32)
    visual_now = visual_blocks.astype(jnp.float32)
    inputs = []
    gathered = []
    saved = []
    for sublayer in range(3):
        inputs.append((text_now, visual_now))
        text_norm = normalize(text_now, norm_gain[2 * sublayer], norm_shift[2 * sublayer]).astype(
            jnp.bfloat16
        )
        visual_norm = normalize(
            visual_now, norm_gain[2 * sublayer + 1], norm_shift[2 * sublayer + 1]
        ).astype(jnp.bfloat16)
        text_rows, visual_rows = (
            lax.all_gather(text_norm, "mp", axis=0, tiled=True),
            lax.all_gather(visual_norm, "mp", axis=0, tiled=True),
        )
        gathered.append((text_rows, visual_rows))
        text_part = None
        visual_part = None
        if sublayer < 2:
            if sublayer == 0:
                text_context, text_saved = attend_context(
                    text_rows, visual_rows, qkv_weight[0], keep_visual
                )
                visual_context, visual_saved = attend_context(
                    visual_rows, text_rows, qkv_weight[1], keep_text
                )
            else:
                text_context, text_saved = attend_context(text_rows, text_rows, qkv_weight[2], None)
                visual_context, visual_saved = attend_context(
                    visual_rows, visual_rows, qkv_weight[3], None
                )
            text_part = linear(text_context, out_weight[2 * sublayer])
            visual_part = linear(visual_context, out_weight[2 * sublayer + 1])
        else:
            text_part, text_saved = feed_forward(text_rows, up_weight[0], down_weight[0])
            visual_part, visual_saved = feed_forward(visual_rows, up_weight[1], down_weight[1])
        text_added, visual_added = (
            lax.psum_scatter(
                text_part.astype(jnp.bfloat16), "mp", scatter_dimension=0, tiled=True
            ).astype(jnp.float32),
            lax.psum_scatter(
                visual_part.astype(jnp.bfloat16), "mp", scatter_dimension=0, tiled=True
            ).astype(jnp.float32),
        )
        saved.append((text_saved, visual_saved))
        text_now = text_now + text_added
        visual_now = visual_now + visual_added
    text_output = text_now.astype(jnp.bfloat16)
    visual_output = visual_now.astype(jnp.bfloat16)
    text_back = text_cotangent.astype(jnp.float32)
    visual_back = visual_cotangent.astype(jnp.float32)
    in_parts = [None, None, None, None]
    out_parts = [None, None, None, None]
    gain_parts = [None, None, None, None, None, None]
    shift_parts = [None, None, None, None, None, None]
    up_grads = None
    down_grads = None
    for sublayer in (2, 1, 0):
        text_branch, visual_branch = (
            lax.all_gather(text_back.astype(jnp.bfloat16), "mp", axis=0, tiled=True),
            lax.all_gather(visual_back.astype(jnp.bfloat16), "mp", axis=0, tiled=True),
        )
        text_rows, visual_rows = gathered[sublayer]
        text_saved, visual_saved = saved[sublayer]
        if sublayer == 2:
            up_text, down_text, text_part = feed_back(
                text_rows, up_weight[0], down_weight[0], text_saved, text_branch
            )
            up_visual, down_visual, visual_part = feed_back(
                visual_rows, up_weight[1], down_weight[1], visual_saved, visual_branch
            )
            up_grads = jnp.stack([up_text, up_visual])
            down_grads = jnp.stack([down_text, down_visual])
        elif sublayer == 1:
            in_parts[2], out_parts[2], query_back, key_back = attend_back(
                text_rows, text_rows, qkv_weight[2], out_weight[2], None, text_saved, text_branch
            )
            text_part = query_back + key_back
            in_parts[3], out_parts[3], query_back, key_back = attend_back(
                visual_rows,
                visual_rows,
                qkv_weight[3],
                out_weight[3],
                None,
                visual_saved,
                visual_branch,
            )
            visual_part = query_back + key_back
        else:
            in_parts[0], out_parts[0], text_query_back, visual_key_back = attend_back(
                text_rows,
                visual_rows,
                qkv_weight[0],
                out_weight[0],
                keep_visual,
                text_saved,
                text_branch,
            )
            in_parts[1], out_parts[1], visual_query_back, text_key_back = attend_back(
                visual_rows,
                text_rows,
                qkv_weight[1],
                out_weight[1],
                keep_text,
                visual_saved,
                visual_branch,
            )
            text_part = text_query_back + text_key_back
            visual_part = visual_query_back + visual_key_back
        text_norm_grad, visual_norm_grad = (
            lax.psum_scatter(
                text_part.astype(jnp.bfloat16), "mp", scatter_dimension=0, tiled=True
            ).astype(jnp.float32),
            lax.psum_scatter(
                visual_part.astype(jnp.bfloat16), "mp", scatter_dimension=0, tiled=True
            ).astype(jnp.float32),
        )
        text_in, visual_in = inputs[sublayer]
        text_pull = jax.vjp(normalize, text_in, norm_gain[2 * sublayer], norm_shift[2 * sublayer])[
            1
        ]
        text_delta, gain_parts[2 * sublayer], shift_parts[2 * sublayer] = text_pull(text_norm_grad)
        visual_pull = jax.vjp(
            normalize, visual_in, norm_gain[2 * sublayer + 1], norm_shift[2 * sublayer + 1]
        )[1]
        visual_delta, gain_parts[2 * sublayer + 1], shift_parts[2 * sublayer + 1] = visual_pull(
            visual_norm_grad
        )
        text_back = text_back + text_delta
        visual_back = visual_back + visual_delta
    gain_grads = jnp.stack(gain_parts)
    shift_grads = jnp.stack(shift_parts)
    gain_grads, shift_grads = (
        lax.psum(gain_grads.astype(jnp.bfloat16), "mp").astype(jnp.float32),
        lax.psum(shift_grads.astype(jnp.bfloat16), "mp").astype(jnp.float32),
    )
    in_grads = jnp.stack(in_parts)
    out_grads = jnp.stack(out_parts)
    in_grads, out_grads, up_grads, down_grads = jax.tree.map(
        lambda grad: lax.psum(grad.astype(jnp.bfloat16), "dp").astype(jnp.float32),
        (in_grads, out_grads, up_grads, down_grads),
    )
    gain_grads, shift_grads = lax.psum((gain_grads, shift_grads), "dp")
    return (
        text_output,
        visual_output,
        text_back.astype(jnp.bfloat16),
        visual_back.astype(jnp.bfloat16),
        in_grads,
        out_grads,
        up_grads,
        down_grads,
        gain_grads,
        shift_grads,
    )


def solution(mesh):
    placed = (
        P(("dp", "mp"), None, None),
        P(("dp", "mp"), None, None),
        P("dp", None),
        P(None, None, None, "mp"),
        P(None, "mp", None),
        P(None, None, "mp"),
        P(None, "mp", None),
        P(),
        P(),
        P(("dp", "mp"), None, None),
        P(("dp", "mp"), None, None),
    )
    return jax.shard_map(
        per_device,
        mesh=mesh,
        in_specs=placed,
        out_specs=(
            P(("dp", "mp"), None, None),
            P(("dp", "mp"), None, None),
            P(("dp", "mp"), None, None),
            P(("dp", "mp"), None, None),
            P(None, None, None, "mp"),
            P(None, "mp", None),
            P(None, None, "mp"),
            P(None, "mp", None),
            P(),
            P(),
        ),
        check_vma=False,
    )
```

profile of v0, /device:TPU:0, one launch (start us, length us, event | category | flops | bytes accessed | tf_op | source)
XLA Modules:
  0.0 1164.1 jit_solution(13793235685979987641)
XLA Ops:
  20.7 18.6 %all-gather.13.cloned.1.call-done = bf16[32,40,768]{2,1,0:T(8,128)(2,1)} async-done(((bf16[8,40,768]{2,1,0:T(8,128)(2,1)}), bf16[32,40,768]{2,1,0:T(8,128)(2,1)}) %all-gather.13.cloned.1.call-update) | async-done | bytes 1966096 | tf_op jit(solution)/shard_map/all_gather | solution.py:173
  42.8 27.1 %all-gather.15.cloned.1.call-done = bf16[32,64,768]{2,1,0:T(8,128)(2,1)} async-done(((bf16[8,64,768]{2,1,0:T(8,128)(2,1)}), bf16[32,64,768]{2,1,0:T(8,128)(2,1)}) %all-gather.15.cloned.1.call-update) | async-done | bytes 3145744 | tf_op jit(solution)/shard_map/all_gather | solution.py:172
  69.9 3.9 convolution_convert_fusion.13
  75.6 4.4 convolution_convert_fusion.14
  100.8 4.1 convolution_convert_fusion.18
  114.1 3.9 convolution_convert_fusion.3
  118.0 5.9 reduce-scatter.19.cloned.1.call-done
  127.7 37.1 %reduce-scatter.13.cloned.1.call-done = bf16[8,64,768]{2,1,0:T(8,128)(2,1)} async-done(((bf16[32,64,768]{2,1,0:T(8,128)(2,1)}), bf16[8,64,768]{2,1,0:T(8,128)(2,1)}) %reduce-scatter.13.cloned.1.call-update) | async-done | bytes 786448 | tf_op jit(solution)/shard_map/reduce_scatter | solution.py:197
  168.6 20.0 %all-gather.21.cloned.1.call-done = bf16[32,40,768]{2,1,0:T(8,128)(2,1)} async-done(((bf16[8,40,768]{2,1,0:T(8,128)(2,1)}), bf16[32,40,768]{2,1,0:T(8,128)(2,1)}) %all-gather.21.cloned.1.call-update) | async-done | bytes 1966096 | tf_op jit(solution)/shard_map/all_gather | solution.py:173
  198.0 3.9 convolution_convert_fusion.26
  244.0 3.9 convolution_convert_fusion.2
  248.0 4.7 reduce-scatter.21.cloned.1.call-done
  256.6 37.1 %reduce-scatter.15.cloned.1.call-done = bf16[8,64,768]{2,1,0:T(8,128)(2,1)} async-done(((bf16[32,64,768]{2,1,0:T(8,128)(2,1)}), bf16[8,64,768]{2,1,0:T(8,128)(2,1)}) %reduce-scatter.15.cloned.1.call-update) | async-done | bytes 786448 | tf_op jit(solution)/shard_map/reduce_scatter | solution.py:197
  297.9 19.9 %all-gather.23.cloned.1.call-done = bf16[32,40,768]{2,1,0:T(8,128)(2,1)} async-done(((bf16[8,40,768]{2,1,0:T(8,128)(2,1)}), bf16[32,40,768]{2,1,0:T(8,128)(2,1)}) %all-gather.23.cloned.1.call-update) | async-done | bytes 1966096 | tf_op jit(solution)/shard_map/all_gather | solution.py:173
  317.7 5.5 fusion.80
  323.2 17.8 %all-gather.31.cloned.1.call-done = bf16[32,40,768]{2,1,0:T(8,128)(2,1)} async-done(((bf16[8,40,768]{2,1,0:T(8,128)(2,1)}), bf16[32,40,768]{2,1,0:T(8,128)(2,1)}) %all-gather.31.cloned.1.call-update) | async-done | bytes 1966096 | tf_op jit(solution)/shard_map/all_gather | solution.py:220
  341.0 7.0 fusion.13
  352.7 18.9 %all-gather.19.cloned.1.call-done = bf16[32,64,768]{2,1,0:T(8,128)(2,1)} async-done(((bf16[8,64,768]{2,1,0:T(8,128)(2,1)}), bf16[32,64,768]{2,1,0:T(8,128)(2,1)}) %all-gather.19.cloned.1.call-update) | async-done | bytes 3145744 | tf_op jit(solution)/shard_map/all_gather | solution.py:172
  371.7 7.5 fusion.85
  379.2 22.4 %all-gather.25.cloned.1.call-done = bf16[32,64,768]{2,1,0:T(8,128)(2,1)} async-done(((bf16[8,64,768]{2,1,0:T(8,128)(2,1)}), bf16[32,64,768]{2,1,0:T(8,128)(2,1)}) %all-gather.25.cloned.1.call-update) | async-done | bytes 3145744 | tf_op jit(solution)/shard_map/all_gather | solution.py:219
  401.7 8.5 fusion.6
  411.8 4.1 convolution_convert_fusion
  415.9 18.7 %reduce-scatter.29.cloned.1.call-done = bf16[8,40,768]{2,1,0:T(8,128)(2,1)} async-done(((bf16[32,40,768]{2,1,0:T(8,128)(2,1)}), bf16[8,40,768]{2,1,0:T(8,128)(2,1)}) %reduce-scatter.29.cloned.1.call-update) | async-done | bytes 491536 | tf_op jit(solution)/shard_map/reduce_scatter | solution.py:273
  439.9 35.0 %reduce-scatter.25.cloned.1.call-done = bf16[8,64,768]{2,1,0:T(8,128)(2,1)} async-done(((bf16[32,64,768]{2,1,0:T(8,128)(2,1)}), bf16[8,64,768]{2,1,0:T(8,128)(2,1)}) %reduce-scatter.25.cloned.1.call-update) | async-done | bytes 786448 | tf_op jit(solution)/shard_map/reduce_scatter | solution.py:270
  479.8 18.9 %all-gather.33.cloned.1.call-done = bf16[32,40,768]{2,1,0:T(8,128)(2,1)} async-done(((bf16[8,40,768]{2,1,0:T(8,128)(2,1)}), bf16[32,40,768]{2,1,0:T(8,128)(2,1)}) %all-gather.33.cloned.1.call-update) | async-done | bytes 1966096 | tf_op jit(solution)/shard_map/all_gather | solution.py:220
  537.0 6.3 convolution_convert_fusion.5
  543.6 4.3 convolution_convert_fusion.12
  550.5 4.2 multiply_reduce_fusion
  561.6 4.0 fusion.36
  578.4 8.7 convolution_convert_fusion.1
  590.3 10.0 reduce-scatter.23.cloned.1.call-done
  600.3 3.9 fusion.209
  608.0 4.5 reshape.443
  616.1 24.6 %reduce-scatter.27.cloned.1.call-done = bf16[8,64,768]{2,1,0:T(8,128)(2,1)} async-done(((bf16[32,64,768]{2,1,0:T(8,128)(2,1)}), bf16[8,64,768]{2,1,0:T(8,128)(2,1)}) %reduce-scatter.27.cloned.1.call-update) | async-done | bytes 786448 | tf_op jit(solution)/shard_map/reduce_scatter | solution.py:270
  643.9 37.2 %reduce-scatter.17.cloned.1.call-done = bf16[8,64,768]{2,1,0:T(8,128)(2,1)} async-done(((bf16[32,64,768]{2,1,0:T(8,128)(2,1)}), bf16[8,64,768]{2,1,0:T(8,128)(2,1)}) %reduce-scatter.17.cloned.1.call-update) | async-done | bytes 786448 | tf_op jit(solution)/shard_map/reduce_scatter | solution.py:197
  681.0 4.1 fusion.210
  685.4 5.1 fusion.44
  699.5 5.5 all-gather.35.cloned.1.call-done
  726.7 9.0 all-gather.29.cloned.1.call-done
  735.7 3.9 fusion.49
  769.6 8.5 fusion.45
  782.5 3.9 convolution_convert_fusion.8
  786.4 5.1 fusion.172
  799.2 4.1 add_convert_fusion
  803.6 5.7 fusion.43
  849.5 10.7 all-reduce.2
  860.2 40.7 %all-reduce = (f32[6,768]{1,0:T(8,128)}, f32[6,768]{1,0:T(8,128)}) all-reduce(bf16[6,768]{1,0:T(8,128)(2,1)S(1)} %get-tuple-element.40, bf16[6,768]{1,0:T(8,128)(2,1)S(1)} %get-tuple-element.41), channel_id=1, replica_groups=mesh['dp'=8,'mp'=4] {'dp'}, use_global_device_ids=true, to_apply=%region_59.0 | all-reduce | flops 9216 | bytes 55296 | tf_op jit(solution)/shard_map/psum | solution.py:302
  903.9 241.7 %all-reduce.5.cloned.1.call-done = (bf16[4,768,3,192]{1,3,2,0:T(8,128)(2,1)}, bf16[4,192,768]{2,1,0:T(8,128)(2,1)}, bf16[2,768,768]{2,1,0:T(8,128)(2,1)}, bf16[2,768,768]{2,1,0:T(8,128)(2,1)}) async-done(((bf16[4,768,3,192]{1,3,2,0:T(8,128)(2,1)}, bf16[4,192,768]{2,1,0:T(8,128)(2,1)}, bf16[2,768,768]{2,1,0:T(8,128)(2,1)}, bf16[2,768,768]{2,1,0:T(8,128)(2,1)}), (bf16[4,768,3,192]{1,3,2,0:T(8,128)(2,1)}, ...) | async-done | bytes 9437200 | tf_op jit(solution)/shard_map/psum | solution.py:299
  (524 shorter events, 333.7 us)
Async XLA Ops:
  7.2 7.4 copy-start
  7.2 32.1 %all-gather.13.cloned.1.call-start = ((), (), s32[]{:S(2)}) async-start(), calls=%async_computation.12 | async-start | bytes 2457600 | tf_op jit(solution)/shard_map/all_gather | solution.py:173
  8.5 6.1 copy-start.95
  14.5 55.4 %all-gather.15.cloned.1.call-start = ((), (), s32[]{:S(2)}) async-start(), calls=%async_computation.13 | async-start | bytes 3932160 | tf_op jit(solution)/shard_map/all_gather | solution.py:172
  14.8 5.8 copy-start.93
  15.2 5.5 copy-start.107
  16.5 107.4 %reduce-scatter.19.cloned.1.call-start = ((), (), s32[]{:S(2)}) async-start(), calls=%async_computation.19 | async-start | bytes 2457600 | tf_op jit(solution)/shard_map/reduce_scatter | solution.py:200
  17.1 68.9 %copy-start.111 = (f32[32]{0:T(128)}, f32[32]{0:T(128)S(1)}, u32[]{:S(2)}) copy-start(f32[32]{0:T(128)S(1)} %get-tuple-element.58) | copy-start | bytes 388
  17.1 92.8 %copy-start.113 = (f32[32]{0:T(128)}, f32[32]{0:T(128)S(1)}, u32[]{:S(2)}) copy-start(f32[32]{0:T(128)S(1)} %get-tuple-element.59) | copy-start | bytes 388
  20.7 49.3 %copy-start.65 = (bf16[768,3,192]{0,2,1:T(8,128)(2,1)}, bf16[768,3,192]{0,2,1:T(8,128)(2,1)S(1)}, u32[]{:S(2)}) copy-start(bf16[768,3,192]{0,2,1:T(8,128)(2,1)S(1)} %get-tuple-element.53) | copy-start | bytes 2654212
  75.6 7.0 copy-start.18
  93.4 71.4 %reduce-scatter.13.cloned.1.call-start = ((), (), s32[]{:S(2)}) async-start(), calls=%async_computation.14 | async-start | bytes 3932160 | tf_op jit(solution)/shard_map/reduce_scatter | solution.py:197
  118.0 5.9 copy-start.3
  118.0 70.6 %all-gather.21.cloned.1.call-start = ((), (), s32[]{:S(2)}) async-start(), calls=%async_computation.20 | async-start | bytes 2457600 | tf_op jit(solution)/shard_map/all_gather | solution.py:173
  127.6 91.5 %all-gather.17.cloned.1.call-start = ((), (), s32[]{:S(2)}) async-start(), calls=%async_computation.15 | async-start | bytes 3932160 | tf_op jit(solution)/shard_map/all_gather | solution.py:172
  166.7 21.9 %copy-start.69 = (bf16[768,3,192]{0,2,1:T(8,128)(2,1)S(1)}, bf16[768,3,192]{0,2,1:T(8,128)(2,1)}, u32[]{:S(2)}) copy-start(bf16[768,3,192]{0,2,1:T(8,128)(2,1)} %get-tuple-element.50) | copy-start | bytes 2654212
  168.1 84.7 %reduce-scatter.21.cloned.1.call-start = ((), (), s32[]{:S(2)}) async-start(), calls=%async_computation.21 | async-start | bytes 2457600 | tf_op jit(solution)/shard_map/reduce_scatter | solution.py:200
  198.0 7.5 copy-start.40
  218.0 75.8 %reduce-scatter.15.cloned.1.call-start = ((), (), s32[]{:S(2)}) async-start(), calls=%async_computation.16 | async-start | bytes 3932160 | tf_op jit(solution)/shard_map/reduce_scatter | solution.py:197
  247.9 69.8 %all-gather.23.cloned.1.call-start = ((), (), s32[]{:S(2)}) async-start(), calls=%async_computation.22 | async-start | bytes 2457600 | tf_op jit(solution)/shard_map/all_gather | solution.py:173
  256.0 85.0 %all-gather.31.cloned.1.call-start = ((), (), s32[]{:S(2)}) async-start(), calls=%async_computation.29 | async-start | bytes 2457600 | tf_op jit(solution)/shard_map/all_gather | solution.py:220
  256.6 115.1 %all-gather.19.cloned.1.call-start = ((), (), s32[]{:S(2)}) async-start(), calls=%async_computation.17 | async-start | bytes 3932160 | tf_op jit(solution)/shard_map/all_gather | solution.py:172
  297.0 104.6 %all-gather.25.cloned.1.call-start = ((), (), s32[]{:S(2)}) async-start(), calls=%async_computation.24 | async-start | bytes 3932160 | tf_op jit(solution)/shard_map/all_gather | solution.py:219
  297.6 137.0 %reduce-scatter.29.cloned.1.call-start = ((), (), s32[]{:S(2)}) async-start(), calls=%async_computation.30 | async-start | bytes 2457600 | tf_op jit(solution)/shard_map/reduce_scatter | solution.py:273
  341.0 8.3 copy-start.122
  352.3 122.6 %reduce-scatter.25.cloned.1.call-start = ((), (), s32[]{:S(2)}) async-start(), calls=%async_computation.25 | async-start | bytes 3932160 | tf_op jit(solution)/shard_map/reduce_scatter | solution.py:270
  401.7 10.1 copy-start.123
  415.9 82.9 %all-gather.33.cloned.1.call-start = ((), (), s32[]{:S(2)}) async-start(), calls=%async_computation.31 | async-start | bytes 2457600 | tf_op jit(solution)/shard_map/all_gather | solution.py:220
  439.9 103.8 %all-gather.27.cloned.1.call-start = ((), (), s32[]{:S(2)}) async-start(), calls=%async_computation.26 | async-start | bytes 3932160 | tf_op jit(solution)/shard_map/all_gather | solution.py:219
  479.6 107.6 %reduce-scatter.31.cloned.1.call-start = ((), (), s32[]{:S(2)}) async-start(), calls=%async_computation.32 | async-start | bytes 2457600 | tf_op jit(solution)/shard_map/reduce_scatter | solution.py:273
  537.0 63.3 %reduce-scatter.23.cloned.1.call-start = ((), (), s32[]{:S(2)}) async-start(), calls=%async_computation.23 | async-start | bytes 2457600 | tf_op jit(solution)/shard_map/reduce_scatter | solution.py:200
  543.3 97.4 %reduce-scatter.27.cloned.1.call-start = ((), (), s32[]{:S(2)}) async-start(), calls=%async_computation.27 | async-start | bytes 3932160 | tf_op jit(solution)/shard_map/reduce_scatter | solution.py:270
  578.0 103.1 %reduce-scatter.17.cloned.1.call-start = ((), (), s32[]{:S(2)}) async-start(), calls=%async_computation.18 | async-start | bytes 3932160 | tf_op jit(solution)/shard_map/reduce_scatter | solution.py:197
  587.1 117.9 %all-gather.35.cloned.1.call-start = ((), (), s32[]{:S(2)}) async-start(), calls=%async_computation.33 | async-start | bytes 2457600 | tf_op jit(solution)/shard_map/all_gather | solution.py:220
  604.2 131.5 %all-gather.29.cloned.1.call-start = ((), (), s32[]{:S(2)}) async-start(), calls=%async_computation.28 | async-start | bytes 3932160 | tf_op jit(solution)/shard_map/all_gather | solution.py:219
  685.2 154.6 %reduce-scatter.35.cloned.1.call-start = ((), (), s32[]{:S(2)}) async-start(), calls=%async_computation.35 | async-start | bytes 2457600 | tf_op jit(solution)/shard_map/reduce_scatter | solution.py:273
  698.2 6.8 copy-start.117
  705.0 7.0 copy-start.5
  705.0 7.0 copy-start.88
  723.0 12.7 %copy-start.116 = (bf16[32]{0:T(256)(128)(2,1)S(1)}, bf16[32]{0:T(256)(128)(2,1)}, u32[]{:S(2)}) copy-start(bf16[32]{0:T(256)(128)(2,1)} %get-tuple-element.57) | copy-start | bytes 196
  767.0 78.4 %reduce-scatter.33.cloned.1.call-start = ((), (), s32[]{:S(2)}) async-start(), calls=%async_computation.34 | async-start | bytes 3932160 | tf_op jit(solution)/shard_map/reduce_scatter | solution.py:270
  769.6 8.5 copy-start.33
  769.6 8.5 copy-start.38
  791.5 7.3 slice-start
  803.4 5.9 copy-start.89
  803.4 342.2 %all-reduce.5.cloned.1.call-start = ((), (), s32[]{:S(2)}) async-start(), calls=%async_computation.36 | async-start | bytes 18874368 | tf_op jit(solution)/shard_map/psum | solution.py:299
  803.6 5.7 copy-start.90
  803.6 5.7 copy-start.91
  (109 other events, 290.3 us)
Sparse Core Ops, SparseCore 0:
  14.7 24.5 all-gather.12
  41.4 28.4 all-gather.14
  93.5 30.3 reduce-scatter.18
  126.9 37.8 reduce-scatter.12
  166.8 21.8 all-gather.20
  190.6 28.4 all-gather.16
  222.3 30.3 reduce-scatter.20
  255.8 37.8 reduce-scatter.14
  295.9 21.8 all-gather.22
  319.2 21.8 all-gather.30
  343.2 28.4 all-gather.18
  373.1 28.4 all-gather.24
  404.2 30.3 reduce-scatter.28
  437.0 37.8 reduce-scatter.24
  476.9 21.8 all-gather.32
  500.8 28.4 all-gather.26
  537.1 30.3 reduce-scatter.30
  569.9 30.3 reduce-scatter.22
  602.8 37.8 reduce-scatter.26
  643.1 37.8 reduce-scatter.16
  683.2 21.8 all-gather.34
  707.2 28.4 all-gather.28
  767.1 30.3 reduce-scatter.34
  803.5 37.7 reduce-scatter.32
  846.3 299.1 all-reduce.4
where the time goes:
time: 1170 us; the launch traced here: 1160 us
  waiting for transfers between devices  633 us (54%)
  matrix products  245 us (21%)
  local copies, waits for them, and re-layouts  130 us (11%)
  other arithmetic  84.9 us (7%)
  blocking collectives  51.5 us (4%)
  between operations  16 us (1%)
    psum x1, waiting for transfers between devices, per_device(): lax.psum(grad.astype(jnp.bfloat16), 'dp').astype(jnp.float32)  242 us
    reduce_scatter x6, waiting for transfers between devices, per_device(): lax.psum_scatter(text_part.astype(jnp.bfloat16), 'mp', scatter_dimension=...  171 us
    dot_general x20, matrix products, linear(): jnp.einsum('pld,de->ple', activation, weight, preferred_element_type=jnp....  82 us
    dot_general x20, matrix products, linear_back(): jnp.einsum('ple,de->pld', gradient, weight, preferred_element_type=jnp.fl...  68.1 us
    all_gather x3, waiting for transfers between devices, per_device(): lax.all_gather(visual_norm, 'mp', axis=0, tiled=True)  58.5 us
    all_gather x3, waiting for transfers between devices, per_device(): lax.all_gather(text_norm, 'mp', axis=0, tiled=True)  47.1 us
    all_gather x3, waiting for transfers between devices, per_device(): lax.all_gather(visual_back.astype(jnp.bfloat16), 'mp', axis=0, tiled=True)  42.2 us
    psum x1, blocking collectives, per_device(): gain_grads, shift_grads = lax.psum((gain_grads, shift_grads), 'dp')  40.7 us
  transfers between devices with their start and end apart: 25, of which 21 were waited for; matrix products, arithmetic and copies ran while one was open for 31% of the time, Pallas kernels for 0%

commit v1 on v0

--- a/solution.py
+++ b/solution.py
@@ -296,7 +296,9 @@
     in_grads = jnp.stack(in_parts)
     out_grads = jnp.stack(out_parts)
     in_grads, out_grads, up_grads, down_grads = jax.tree.map(
-        lambda grad: lax.psum(grad.astype(jnp.bfloat16), "dp").astype(jnp.float32),
+        lambda grad: jnp.sum(lax.all_gather(grad.astype(jnp.bfloat16), "dp"), axis=0).astype(
+            jnp.float32
+        ),
         (in_grads, out_grads, up_grads, down_grads),
     )
     gain_grads, shift_grads = lax.psum((gain_grads, shift_grads), "dp")

time: 1170 us -> 2290 us (1.96)
  waiting for transfers between devices: 633 us -> 1680 us
  other arithmetic: 84.9 us -> 134 us
    all_gather x0 -> x4, waiting for transfers between devices: none -> 1270 us  [per_device(): lax.all_gather(grad.astype(jnp.bfloat16), 'dp')]
    psum x1 -> x0, waiting for transfers between devices: 242 us -> none  [per_device(): lax.psum(grad.astype(jnp.bfloat16), 'dp').astype(jnp.float32)]
    reduce_sum x0 -> x4, other arithmetic: none -> 46.1 us  [per_device(): jnp.sum(lax.all_gather(grad.astype(jnp.bfloat16), 'dp'), axis=0)]
  transfers between devices with their start and end apart: 25 -> 28, of which waited for: 21 -> 24; matrix products, arithmetic and copies ran while one was open for 31% -> 17% of each run, Pallas kernels for 0% -> 0%
where the time goes in v1:
time: 2290 us; the launch traced here: 2280 us
  waiting for transfers between devices  1680 us (73%)
  matrix products  244 us (11%)
  other arithmetic  134 us (6%)
  local copies, waits for them, and re-layouts  133 us (6%)
  blocking collectives  61.2 us (3%)
    all_gather x4, waiting for transfers between devices, per_device(): lax.all_gather(grad.astype(jnp.bfloat16), 'dp')  1270 us
    reduce_scatter x6, waiting for transfers between devices, per_device(): lax.psum_scatter(text_part.astype(jnp.bfloat16), 'mp', scatter_dimension=...  181 us
    dot_general x20, matrix products, linear(): jnp.einsum('pld,de->ple', activation, weight, preferred_element_type=jnp....  82 us
    dot_general x20, matrix products, linear_back(): jnp.einsum('ple,de->pld', gradient, weight, preferred_element_type=jnp.fl...  68 us
    all_gather x3, waiting for transfers between devices, per_device(): lax.all_gather(visual_norm, 'mp', axis=0, tiled=True)  56.6 us
    all_gather x3, waiting for transfers between devices, per_device(): lax.all_gather(visual_back.astype(jnp.bfloat16), 'mp', axis=0, tiled=True)  55.9 us
    psum x1, blocking collectives, per_device(): gain_grads, shift_grads = lax.psum((gain_grads, shift_grads), 'dp')  50 us
    all_gather x3, waiting for transfers between devices, per_device(): lax.all_gather(text_norm, 'mp', axis=0, tiled=True)  47 us
  transfers between devices with their start and end apart: 28, of which 24 were waited for; matrix products, arithmetic and copies ran while one was open for 17% of the time, Pallas kernels for 0%

profile of v1, /device:TPU:0, one launch (start us, length us, event | category | flops | bytes accessed | tf_op | source)
XLA Modules:
  0.0 2277.5 jit_solution(3527688606395060996)
XLA Ops:
  20.7 18.6 all-gather.17.cloned.1.call-done
  42.8 27.2 %all-gather.19.cloned.1.call-done = bf16[32,64,768]{2,1,0:T(8,128)(2,1)} async-done(((bf16[8,64,768]{2,1,0:T(8,128)(2,1)}), bf16[32,64,768]{2,1,0:T(8,128)(2,1)}) %all-gather.19.cloned.1.call-update) | async-done | bytes 3145744 | tf_op jit(solution)/shard_map/all_gather | solution.py:172
  75.7 4.4 convolution_convert_fusion.14
  100.9 4.1 convolution_convert_fusion.18
  118.1 5.9 reduce-scatter.19.cloned.1.call-done
  127.8 37.1 %reduce-scatter.13.cloned.1.call-done = bf16[8,64,768]{2,1,0:T(8,128)(2,1)} async-done(((bf16[32,64,768]{2,1,0:T(8,128)(2,1)}), bf16[8,64,768]{2,1,0:T(8,128)(2,1)}) %reduce-scatter.13.cloned.1.call-update) | async-done | bytes 786448 | tf_op jit(solution)/shard_map/reduce_scatter | solution.py:197
  168.8 20.0 all-gather.25.cloned.1.call-done
  248.1 4.7 reduce-scatter.21.cloned.1.call-done
  257.3 36.5 %reduce-scatter.15.cloned.1.call-done = bf16[8,64,768]{2,1,0:T(8,128)(2,1)} async-done(((bf16[32,64,768]{2,1,0:T(8,128)(2,1)}), bf16[8,64,768]{2,1,0:T(8,128)(2,1)}) %reduce-scatter.15.cloned.1.call-update) | async-done | bytes 786448 | tf_op jit(solution)/shard_map/reduce_scatter | solution.py:197
  299.8 18.0 all-gather.27.cloned.1.call-done
  317.8 5.5 fusion.80
  323.3 17.8 all-gather.35.cloned.1.call-done
  341.1 7.0 fusion.13
  353.0 18.8 all-gather.23.cloned.1.call-done
  371.8 7.5 fusion.85
  379.3 22.4 all-gather.29.cloned.1.call-done
  401.7 8.5 fusion.6
  416.0 18.7 reduce-scatter.29.cloned.1.call-done
  441.3 33.7 %reduce-scatter.25.cloned.1.call-done = bf16[8,64,768]{2,1,0:T(8,128)(2,1)} async-done(((bf16[32,64,768]{2,1,0:T(8,128)(2,1)}), bf16[8,64,768]{2,1,0:T(8,128)(2,1)}) %reduce-scatter.25.cloned.1.call-update) | async-done | bytes 786448 | tf_op jit(solution)/shard_map/reduce_scatter | solution.py:270
  480.5 18.3 all-gather.37.cloned.1.call-done
  537.0 6.3 convolution_convert_fusion.5
  543.6 4.3 convolution_convert_fusion.12
  550.5 4.2 multiply_reduce_fusion
  561.7 4.1 fusion.36
  578.5 8.6 convolution_convert_fusion.1
  591.0 9.2 reduce-scatter.23.cloned.1.call-done
  604.2 37.0 %reduce-scatter.27.cloned.1.call-done = bf16[8,64,768]{2,1,0:T(8,128)(2,1)} async-done(((bf16[32,64,768]{2,1,0:T(8,128)(2,1)}), bf16[8,64,768]{2,1,0:T(8,128)(2,1)}) %reduce-scatter.27.cloned.1.call-update) | async-done | bytes 786448 | tf_op jit(solution)/shard_map/reduce_scatter | solution.py:270
  644.4 37.1 %reduce-scatter.17.cloned.1.call-done = bf16[8,64,768]{2,1,0:T(8,128)(2,1)} async-done(((bf16[32,64,768]{2,1,0:T(8,128)(2,1)}), bf16[8,64,768]{2,1,0:T(8,128)(2,1)}) %reduce-scatter.17.cloned.1.call-update) | async-done | bytes 786448 | tf_op jit(solution)/shard_map/reduce_scatter | solution.py:197
  681.5 4.1 fusion.210
  685.7 19.8 all-gather.39.cloned.1.call-done
  727.2 9.0 all-gather.33.cloned.1.call-done
  777.7 5.0 fusion.172
  790.5 4.1 add_convert_fusion
  805.5 4.6 fusion.46
  810.2 6.2 fusion.45
  872.6 11.2 all-reduce.1
  883.8 50.0 %all-reduce = (f32[6,768]{1,0:T(8,128)}, f32[6,768]{1,0:T(8,128)}) all-reduce(bf16[6,768]{1,0:T(8,128)(2,1)S(1)} %get-tuple-element.36, bf16[6,768]{1,0:T(8,128)(2,1)S(1)} %get-tuple-element.37), channel_id=1, replica_groups=mesh['dp'=8,'mp'=4] {'dp'}, use_global_device_ids=true, to_apply=%region_59.0 | all-reduce | flops 9216 | bytes 55296 | tf_op jit(solution)/shard_map/psum | solution.py:304
  936.7 269.1 %all-gather.45.cloned.1.call-done = bf16[8,2,768,768]{3,2,1,0:T(8,128)(2,1)} async-done(((bf16[1,2,768,768]{3,2,1,0:T(8,128)(2,1)}), bf16[8,2,768,768]{3,2,1,0:T(8,128)(2,1)}) %all-gather.45.cloned.1.call-update) | async-done | bytes 18874384 | tf_op jit(solution)/shard_map/all_gather | solution.py:299
  1205.8 12.4 reduce_sum.499
  1218.2 4.2 convert_element_type.614
  1222.4 347.2 %all-gather.47.cloned.1.call-done = bf16[8,2,768,768]{3,2,1,0:T(8,128)(2,1)} async-done(((bf16[1,2,768,768]{3,2,1,0:T(8,128)(2,1)}), bf16[8,2,768,768]{3,2,1,0:T(8,128)(2,1)}) %all-gather.47.cloned.1.call-update) | async-done | bytes 18874384 | tf_op jit(solution)/shard_map/all_gather | solution.py:299
  1569.5 12.3 reduce_sum.503
  1581.8 4.2 convert_element_type.615
  1586.1 122.8 %all-gather.43.cloned.1.call-done = bf16[8,4,192,768]{3,2,1,0:T(8,128)(2,1)} async-done(((bf16[1,4,192,768]{3,2,1,0:T(8,128)(2,1)}), bf16[8,4,192,768]{3,2,1,0:T(8,128)(2,1)}) %all-gather.43.cloned.1.call-update) | async-done | bytes 9437200 | tf_op jit(solution)/shard_map/all_gather | solution.py:299
  1708.8 5.2 reduce_sum.498
  1715.6 532.9 %all-gather.41.cloned.1.call-done = bf16[8,4,768,3,192]{2,4,3,1,0:T(8,128)(2,1)} async-done(((bf16[1,4,768,3,192]{2,4,3,1,0:T(8,128)(2,1)}), bf16[8,4,768,3,192]{2,4,3,1,0:T(8,128)(2,1)}) %all-gather.41.cloned.1.call-update) | async-done | bytes 28311568 | tf_op jit(solution)/shard_map/all_gather | solution.py:299
  2248.5 16.2 reduce_sum.497
  2264.7 5.7 convert_element_type.610
  (586 shorter events, 369.1 us)
Async XLA Ops:
  7.2 32.1 %all-gather.17.cloned.1.call-start = ((), (), s32[]{:S(2)}) async-start(), calls=%async_computation.12 | async-start | bytes 2457600 | tf_op jit(solution)/shard_map/all_gather | solution.py:173
  10.9 115.8 %copy-start.101 = (f32[768]{0:T(1024)}, f32[768]{0:T(1024)S(1)}, u32[]{:S(2)}) copy-start(f32[768]{0:T(1024)S(1)} %get-tuple-element.27) | copy-start | bytes 9220
  10.9 156.0 %copy-start.96 = (f32[768]{0:T(1024)}, f32[768]{0:T(1024)S(1)}, u32[]{:S(2)}) copy-start(f32[768]{0:T(1024)S(1)} %get-tuple-element.24) | copy-start | bytes 9220
  10.9 244.1 %copy-start.86 = (f32[768]{0:T(1024)}, f32[768]{0:T(1024)S(1)}, u32[]{:S(2)}) copy-start(f32[768]{0:T(1024)S(1)} %get-tuple-element.22) | copy-start | bytes 9220
  14.6 55.4 %all-gather.19.cloned.1.call-start = ((), (), s32[]{:S(2)}) async-start(), calls=%async_computation.13 | async-start | bytes 3932160 | tf_op jit(solution)/shard_map/all_gather | solution.py:172
  16.5 107.4 %reduce-scatter.19.cloned.1.call-start = ((), (), s32[]{:S(2)}) async-start(), calls=%async_computation.19 | async-start | bytes 2457600 | tf_op jit(solution)/shard_map/reduce_scatter | solution.py:200
  17.1 69.0 %copy-start.133 = (f32[32]{0:T(128)}, f32[32]{0:T(128)S(1)}, u32[]{:S(2)}) copy-start(f32[32]{0:T(128)S(1)} %get-tuple-element.54) | copy-start | bytes 388
  17.1 93.0 %copy-start.135 = (f32[32]{0:T(128)}, f32[32]{0:T(128)S(1)}, u32[]{:S(2)}) copy-start(f32[32]{0:T(128)S(1)} %get-tuple-element.55) | copy-start | bytes 388
  20.7 49.3 %copy-start.61 = (bf16[768,3,192]{0,2,1:T(8,128)(2,1)}, bf16[768,3,192]{0,2,1:T(8,128)(2,1)S(1)}, u32[]{:S(2)}) copy-start(bf16[768,3,192]{0,2,1:T(8,128)(2,1)S(1)} %get-tuple-element.49) | copy-start | bytes 2654212
  93.4 71.4 %reduce-scatter.13.cloned.1.call-start = ((), (), s32[]{:S(2)}) async-start(), calls=%async_computation.14 | async-start | bytes 3932160 | tf_op jit(solution)/shard_map/reduce_scatter | solution.py:197
  118.1 70.6 %all-gather.25.cloned.1.call-start = ((), (), s32[]{:S(2)}) async-start(), calls=%async_computation.20 | async-start | bytes 2457600 | tf_op jit(solution)/shard_map/all_gather | solution.py:173
  125.3 41.1 %copy-start.84 = (f32[8,40]{1,0:T(8,128)}, f32[8,40]{1,0:T(8,128)S(1)}, u32[]{:S(2)}) copy-start(f32[8,40]{1,0:T(8,128)S(1)} %broadcast_multiply_fusion.4) | copy-start | bytes 3844
  126.6 38.2 %copy-start.123 = (f32[8,40]{1,0:T(8,128)}, f32[8,40]{1,0:T(8,128)S(1)}, u32[]{:S(2)}) copy-start(f32[8,40]{1,0:T(8,128)S(1)} %multiply_reduce_fusion.11) | copy-start | bytes 3844
  126.6 40.2 %copy-start.113 = (f32[8,40]{1,0:T(8,128)}, f32[8,40]{1,0:T(8,128)S(1)}, u32[]{:S(2)}) copy-start(f32[8,40]{1,0:T(8,128)S(1)} %fusion.195) | copy-start | bytes 3844
  127.7 91.5 %all-gather.21.cloned.1.call-start = ((), (), s32[]{:S(2)}) async-start(), calls=%async_computation.15 | async-start | bytes 3932160 | tf_op jit(solution)/shard_map/all_gather | solution.py:172
  166.8 24.2 %copy-start.121 = (f32[8,64]{1,0:T(8,128)}, f32[8,64]{1,0:T(8,128)S(1)}, u32[]{:S(2)}) copy-start(f32[8,64]{1,0:T(8,128)S(1)} %multiply_reduce_fusion.9) | copy-start | bytes 6148
  166.8 21.9 copy-start.65
  166.8 24.2 %copy-start.109 = (f32[8,64]{1,0:T(8,128)}, f32[8,64]{1,0:T(8,128)S(1)}, u32[]{:S(2)}) copy-start(f32[8,64]{1,0:T(8,128)S(1)} %fusion.193) | copy-start | bytes 6148
  168.2 84.6 %reduce-scatter.21.cloned.1.call-start = ((), (), s32[]{:S(2)}) async-start(), calls=%async_computation.21 | async-start | bytes 2457600 | tf_op jit(solution)/shard_map/reduce_scatter | solution.py:200
  218.0 75.8 %reduce-scatter.15.cloned.1.call-start = ((), (), s32[]{:S(2)}) async-start(), calls=%async_computation.16 | async-start | bytes 3932160 | tf_op jit(solution)/shard_map/reduce_scatter | solution.py:197
  248.0 69.8 %all-gather.27.cloned.1.call-start = ((), (), s32[]{:S(2)}) async-start(), calls=%async_computation.22 | async-start | bytes 2457600 | tf_op jit(solution)/shard_map/all_gather | solution.py:173
  256.6 84.5 %all-gather.35.cloned.1.call-start = ((), (), s32[]{:S(2)}) async-start(), calls=%async_computation.29 | async-start | bytes 2457600 | tf_op jit(solution)/shard_map/all_gather | solution.py:220
  257.2 114.6 %all-gather.23.cloned.1.call-start = ((), (), s32[]{:S(2)}) async-start(), calls=%async_computation.17 | async-start | bytes 3932160 | tf_op jit(solution)/shard_map/all_gather | solution.py:172
  299.0 102.8 %all-gather.29.cloned.1.call-start = ((), (), s32[]{:S(2)}) async-start(), calls=%async_computation.24 | async-start | bytes 3932160 | tf_op jit(solution)/shard_map/all_gather | solution.py:219
  299.6 135.2 %reduce-scatter.29.cloned.1.call-start = ((), (), s32[]{:S(2)}) async-start(), calls=%async_computation.30 | async-start | bytes 2457600 | tf_op jit(solution)/shard_map/reduce_scatter | solution.py:273
  352.5 122.5 %reduce-scatter.25.cloned.1.call-start = ((), (), s32[]{:S(2)}) async-start(), calls=%async_computation.25 | async-start | bytes 3932160 | tf_op jit(solution)/shard_map/reduce_scatter | solution.py:270
  415.9 82.9 %all-gather.37.cloned.1.call-start = ((), (), s32[]{:S(2)}) async-start(), calls=%async_computation.31 | async-start | bytes 2457600 | tf_op jit(solution)/shard_map/all_gather | solution.py:220
  441.2 102.4 %all-gather.31.cloned.1.call-start = ((), (), s32[]{:S(2)}) async-start(), calls=%async_computation.26 | async-start | bytes 3932160 | tf_op jit(solution)/shard_map/all_gather | solution.py:219
  480.3 107.0 %reduce-scatter.31.cloned.1.call-start = ((), (), s32[]{:S(2)}) async-start(), calls=%async_computation.32 | async-start | bytes 2457600 | tf_op jit(solution)/shard_map/reduce_scatter | solution.py:273
  536.9 63.3 %reduce-scatter.23.cloned.1.call-start = ((), (), s32[]{:S(2)}) async-start(), calls=%async_computation.23 | async-start | bytes 2457600 | tf_op jit(solution)/shard_map/reduce_scatter | solution.py:200
  543.3 97.9 %reduce-scatter.27.cloned.1.call-start = ((), (), s32[]{:S(2)}) async-start(), calls=%async_computation.27 | async-start | bytes 3932160 | tf_op jit(solution)/shard_map/reduce_scatter | solution.py:270
  578.1 103.4 %reduce-scatter.17.cloned.1.call-start = ((), (), s32[]{:S(2)}) async-start(), calls=%async_computation.18 | async-start | bytes 3932160 | tf_op jit(solution)/shard_map/reduce_scatter | solution.py:197
  587.2 13.0 copy-start.88
  587.3 118.3 %all-gather.39.cloned.1.call-start = ((), (), s32[]{:S(2)}) async-start(), calls=%async_computation.33 | async-start | bytes 2457600 | tf_op jit(solution)/shard_map/all_gather | solution.py:220
  591.0 50.2 %copy-start.97 = (f32[768]{0:T(1024)S(1)}, f32[768]{0:T(1024)}, u32[]{:S(2)}) copy-start(f32[768]{0:T(1024)} %copy-done.96) | copy-start | bytes 9220
  604.1 39.1 %copy-start.122 = (f32[8,64]{1,0:T(8,128)S(1)}, f32[8,64]{1,0:T(8,128)}, u32[]{:S(2)}) copy-start(f32[8,64]{1,0:T(8,128)} %copy-done.121) | copy-start | bytes 6148
  604.1 39.2 %copy-start.110 = (f32[8,64]{1,0:T(8,128)S(1)}, f32[8,64]{1,0:T(8,128)}, u32[]{:S(2)}) copy-start(f32[8,64]{1,0:T(8,128)} %copy-done.109) | copy-start | bytes 6148
  604.1 77.4 %copy-start.91 = (f32[8,64]{1,0:T(8,128)S(1)}, f32[8,64]{1,0:T(8,128)}, u32[]{:S(2)}) copy-start(f32[8,64]{1,0:T(8,128)} %copy-done.89) | copy-start | bytes 6148
  604.1 77.4 %copy-start.104 = (f32[8,64]{1,0:T(8,128)S(1)}, f32[8,64]{1,0:T(8,128)}, u32[]{:S(2)}) copy-start(f32[8,64]{1,0:T(8,128)} %copy-done.103) | copy-start | bytes 6148
  604.2 77.4 %copy-start.116 = (f32[8,64]{1,0:T(8,128)S(1)}, f32[8,64]{1,0:T(8,128)}, u32[]{:S(2)}) copy-start(f32[8,64]{1,0:T(8,128)} %copy-done.115) | copy-start | bytes 6148
  604.2 132.0 %all-gather.33.cloned.1.call-start = ((), (), s32[]{:S(2)}) async-start(), calls=%async_computation.28 | async-start | bytes 3932160 | tf_op jit(solution)/shard_map/all_gather | solution.py:219
  644.4 61.1 %copy-start.139 = (bf16[32]{0:T(256)(128)(2,1)S(1)}, bf16[32]{0:T(256)(128)(2,1)}, u32[]{:S(2)}) copy-start(bf16[32]{0:T(256)(128)(2,1)} %get-tuple-element.52) | copy-start | bytes 196
  685.7 177.2 %reduce-scatter.35.cloned.1.call-start = ((), (), s32[]{:S(2)}) async-start(), calls=%async_computation.35 | async-start | bytes 2457600 | tf_op jit(solution)/shard_map/reduce_scatter | solution.py:273
  767.4 101.1 %reduce-scatter.33.cloned.1.call-start = ((), (), s32[]{:S(2)}) async-start(), calls=%async_computation.34 | async-start | bytes 3932160 | tf_op jit(solution)/shard_map/reduce_scatter | solution.py:270
  794.6 411.1 %all-gather.45.cloned.1.call-start = ((), (), s32[]{:S(2)}) async-start(), calls=%async_computation.38 | async-start | bytes 21233664 | tf_op jit(solution)/shard_map/all_gather | solution.py:299
  804.0 765.5 %all-gather.47.cloned.1.call-start = ((), (), s32[]{:S(2)}) async-start(), calls=%async_computation.39 | async-start | bytes 21233664 | tf_op jit(solution)/shard_map/all_gather | solution.py:299
  818.0 890.8 %all-gather.43.cloned.1.call-start = ((), (), s32[]{:S(2)}) async-start(), calls=%async_computation.37 | async-start | bytes 10616832 | tf_op jit(solution)/shard_map/all_gather | solution.py:299
  838.5 1410.0 %all-gather.41.cloned.1.call-start = ((), (), s32[]{:S(2)}) async-start(), calls=%async_computation.36 | async-start | bytes 31850496 | tf_op jit(solution)/shard_map/all_gather | solution.py:299
  (136 other events, 457.1 us)
Sparse Core Ops, SparseCore 0:
  14.7 24.5 all-gather.16
  41.4 28.4 all-gather.18
  93.6 30.3 reduce-scatter.18
  126.9 37.8 reduce-scatter.12
  166.8 21.8 all-gather.24
  190.7 28.4 all-gather.20
  222.4 30.3 reduce-scatter.20
  255.9 37.8 reduce-scatter.14
  296.0 21.8 all-gather.26
  319.2 21.8 all-gather.34
  343.2 28.4 all-gather.22
  373.2 28.4 all-gather.28
  404.3 30.3 reduce-scatter.28
  437.1 37.8 reduce-scatter.24
  477.0 21.8 all-gather.36
  500.9 28.4 all-gather.30
  537.0 30.3 reduce-scatter.30
  569.8 30.3 reduce-scatter.22
  603.3 37.8 reduce-scatter.26
  643.6 37.8 reduce-scatter.16
  683.7 21.8 all-gather.38
  707.6 28.4 all-gather.32
  767.5 30.3 reduce-scatter.34
  800.9 37.8 reduce-scatter.32
  840.9 364.8 all-gather.44
  1207.1 362.3 all-gather.46
  1571.6 137.1 all-gather.42
  1710.9 537.5 all-gather.40
